TPU v7x, 512 devices: a whole 4x8x8 slice. The times are simulated.
512 devices in a mesh: fsdp: 16 (over y, x_lo), ed: 32 (over x_hi, z, core).
Axes of the slice: x: 4 (x_hi: 2, x_lo: 2; x = x_hi * 2 + x_lo), y: 8, z: 8, core: 2. Of those that a mesh axis runs over, the one named last changes fastest.
Arguments:
- tokens: bfloat16 [9216, 6144], P('ed', 'fsdp'), may hold values from -6 to 6
- expert_ids: int32 [9216, 2], P('ed'), may hold values from 0 to 7, all different within a row; in each aligned block of 288 rows (0 to 287, 288 to 575, ...) at most 81 rows name the same one
- route_weights: float32 [9216, 2], P('ed'), may hold values from 0.1 to 1
- w_gate: bfloat16 [1, 6144, 8192], P(None, 'fsdp', 'ed'), may hold values from -0.078125 to 0.078125
- w_up: bfloat16 [1, 6144, 8192], P(None, 'fsdp', 'ed'), may hold values from -0.078125 to 0.078125
- w_down: bfloat16 [1, 8192, 6144], P(None, 'ed', 'fsdp'), may hold values from -0.0625 to 0.0625
Outputs:
- mixed: bfloat16 [9216, 6144], P('ed', 'fsdp')
Inputs may be any that keep to these rules, and one draw needn't show every extreme that they name: `expert_ids`: each row names two different experts. In each block of 288 rows that one index of ed holds, no expert is named by more than 81 rows, a bound that some block reaches.
All inputs are finite; a program needn't handle non-finite values.
Results may differ from a plain program's by a relative error of at most 0.025.
Values may be sent and summed in bfloat16 or wider, within the bound.
A program may use at most 64 MiB of HBM per device.

v0:
```python
import jax
import jax.numpy as jnp
from jax import lax
from jax.sharding import PartitionSpec as P

CAP = 81


def slot_match(routes, window, capacity):
    window_ids = jnp.arange(window, dtype=jnp.int32)
    routed = jnp.any(routes[:, :, None, :] == window_ids[None, None, :, None], axis=3)
    position = jnp.cumsum(routed.astype(jnp.int32), axis=1) - 1
    slot_ids = jnp.arange(capacity, dtype=jnp.int32)
    hits = routed[:, :, :, None] & (position[:, :, :, None] == slot_ids[None, None, None, :])
    return hits.astype(jnp.int32)


def take_block(block_rows, row_list):
    return jnp.take(block_rows, row_list, axis=0)


def pick_rows(blocks, routes, window, capacity):
    match = slot_match(routes, window, capacity)
    row_numbers = jnp.arange(blocks.shape[1], dtype=jnp.int32)
    source_row = jnp.sum(match * row_numbers[None, :, None, None], axis=1).reshape(
        blocks.shape[0], window * capacity
    )
    filled = jnp.sum(match, axis=1).reshape(blocks.shape[0], window * capacity)
    picked = jax.vmap(take_block)(blocks, source_row)
    picked = jnp.where(filled[:, :, None] > 0, picked, jnp.zeros_like(picked))
    return picked.reshape(blocks.shape[0], window, capacity, blocks.shape[2])


def combine_matrix(routes, weights, window, capacity):
    match = slot_match(routes[None], window, capacity)[0]
    window_ids = jnp.arange(window, dtype=jnp.int32)
    per_expert = jnp.sum(
        jnp.where(
            routes[:, None, :] == window_ids[None, :, None],
            weights[:, None, :],
            jnp.zeros_like(weights[:, None, :]),
        ),
        axis=2,
    )
    return (per_expert[:, :, None] * match.astype(weights.dtype)).reshape(
        routes.shape[0], window * capacity
    )


def local(tokens, expert_ids, route_weights, w_gate, w_up, w_down):
    window = w_gate.shape[0]
    features_dev = tokens.shape[1]
    hidden_dev = w_gate.shape[2]
    n_ed = lax.axis_size("ed")
    own_slots = pick_rows(tokens[None], expert_ids[None], window, CAP)[0, 0]
    selected = lax.all_gather(own_slots, "ed", axis=0, tiled=True)
    both = jnp.concatenate([w_gate[0], w_up[0]], axis=1)
    partial = jnp.dot(selected, both, preferred_element_type=jnp.float32)
    n_fsdp = lax.axis_size("fsdp")
    rows = partial.shape[0]
    band = -(-rows // (8 * n_fsdp)) * 8
    partial = jnp.pad(partial, ((0, band * n_fsdp - rows), (0, 0)))
    summed = lax.psum_scatter(partial, "fsdp", scatter_dimension=0, tiled=True)
    gate_part = summed[:, :hidden_dev]
    up_part = summed[:, hidden_dev:]
    activation = (jax.nn.silu(gate_part) * up_part).astype(jnp.bfloat16)
    act_rows = lax.all_gather(activation, "fsdp", axis=0, tiled=True)[:rows]
    term = jnp.dot(act_rows, w_down[0], preferred_element_type=jnp.float32)
    term = term.astype(jnp.bfloat16).reshape(n_ed, CAP, features_dev)
    arrived = lax.all_to_all(term, "ed", split_axis=0, concat_axis=0, tiled=True)
    slot_out = jnp.sum(arrived.astype(jnp.float32), axis=0)
    weights_matrix = combine_matrix(expert_ids, route_weights, window, CAP)
    mixed = jnp.dot(
        weights_matrix,
        slot_out.reshape(window * CAP, features_dev),
        precision=lax.Precision.HIGHEST,
        preferred_element_type=jnp.float32,
    )
    return mixed.astype(jnp.bfloat16)


def solution(mesh):
    return jax.shard_map(
        local,
        mesh=mesh,
        in_specs=(
            P("ed", "fsdp"),
            P("ed", None),
            P("ed", None),
            P(None, "fsdp", "ed"),
            P(None, "fsdp", "ed"),
            P(None, "ed", "fsdp"),
        ),
        out_specs=P("ed", "fsdp"),
        check_vma=False,
    )
```

profile of v0, /device:TPU:64, one launch (start us, length us, event | category | flops | bytes accessed | tf_op | source)
XLA Modules:
  0.0 386.1 jit_solution(4538146092871331298)
XLA Ops:
  6.5 0.7 fusion.18
  7.3 0.3 reduce-window.6
  7.6 0.2 slice_reduce_fusion
  7.8 0.2 reduce-window.9
  8.0 0.1 broadcast.184
  8.1 3.0 convert_reduce_fusion.1
  11.1 1.3 gather_fusion
  12.4 0.7 select_bitcast_fusion
  13.2 0.0 all-gather.6.cloned.1.call-update
  13.2 0.0 reduce-scatter.2.cloned.1.call-start
  13.3 89.2 %all-gather.6.cloned.1.call-done = bf16[32,81,384]{2,1,0:T(8,128)(2,1)} async-done(((bf16[1,81,384]{2,1,0:T(8,128)(2,1)}), bf16[32,81,384]{2,1,0:T(8,128)(2,1)}) %all-gather.6.cloned.1.call-update) | async-done | bytes 1990672 | tf_op jit(solution)/shard_map/all_gather | solution.py:56
  102.5 1.9 reshape.322
  104.4 1.5 fusion.1
  106.0 3.0 pad.9
  109.0 0.0 all-gather.4.cloned.1.call-start
  109.0 125.5 %reduce-scatter.2.cloned.1.call-done = f32[168,512]{1,0:T(8,128)} async-done(((f32[2688,512]{1,0:T(8,128)}), f32[168,512]{1,0:T(8,128)}) %reduce-scatter.2.cloned.1.call-update) | async-done | bytes 344080 | tf_op jit(solution)/shard_map/reduce_scatter | solution.py:63
  234.5 1.7 fusion.6
  236.2 73.1 %all-gather.4.cloned.1.call-done = bf16[2688,256]{1,0:T(8,128)(2,1)} async-done(((bf16[168,256]{1,0:T(8,128)(2,1)}), bf16[2688,256]{1,0:T(8,128)(2,1)}) %all-gather.4.cloned.1.call-update) | async-done | bytes 1376272 | tf_op jit(solution)/shard_map/all_gather | solution.py:67
  309.3 2.2 convolution_convert_fusion
  311.5 1.7 reshape.310
  313.2 10.5 %all-to-all-start = ((bf16[32,81,384]{2,1,0:T(8,128)(2,1)}), bf16[32,81,384]{2,1,0:T(8,128)(2,1)S(1)}, u32[]{:S(2)}, u32[]{:S(2)}) async-start(bf16[32,81,384]{2,1,0:T(8,128)(2,1)} %reshape.310), calls=%async_computation.1 | async-start | bytes 4325376 | tf_op jit(solution)/shard_map/all_to_all | solution.py:70
  323.7 54.3 %all-to-all-done = bf16[32,81,384]{2,1,0:T(8,128)(2,1)S(1)} async-done(((bf16[32,81,384]{2,1,0:T(8,128)(2,1)}), bf16[32,81,384]{2,1,0:T(8,128)(2,1)S(1)}, u32[]{:S(2)}, u32[]{:S(2)}) %all-to-all-start) | async-done | bytes 1990688 | tf_op jit(solution)/shard_map/all_to_all | solution.py:70
  378.0 0.3 convert_reduce_fusion
  378.3 1.3 convolution_convert_fusion.1
  (26 shorter events, 0.2 us)
Async XLA Ops:
  6.5 4.6 %copy-start = (bf16[288,384]{1,0:T(8,128)(2,1)S(1)}, bf16[288,384]{1,0:T(8,128)(2,1)}, u32[]{:S(2)}) copy-start(bf16[288,384]{1,0:T(8,128)(2,1)} %param.6) | copy-start | bytes 663556
  6.5 96.0 %all-gather.6.cloned.1.call-start = ((), (), s32[]{:S(2)}) async-start(), calls=%async_computation.4 | async-start | bytes 2230272 | tf_op jit(solution)/shard_map/all_gather | solution.py:56
  13.2 91.2 %copy-start.1 = (bf16[1,384,256]{2,1,0:T(8,128)(2,1)S(1)}, bf16[1,384,256]{2,1,0:T(8,128)(2,1)}, u32[]{:S(2)}) copy-start(bf16[1,384,256]{2,1,0:T(8,128)(2,1)} %param.10) | copy-start | bytes 589828
  13.2 91.2 %copy-start.2 = (bf16[1,384,256]{2,1,0:T(8,128)(2,1)S(1)}, bf16[1,384,256]{2,1,0:T(8,128)(2,1)}, u32[]{:S(2)}) copy-start(bf16[1,384,256]{2,1,0:T(8,128)(2,1)} %param.9) | copy-start | bytes 589828
  13.2 221.3 %reduce-scatter.2.cloned.1.call-start = ((), (), s32[]{:S(2)}) async-start(), calls=%async_computation.2 | async-start | bytes 5849088 | tf_op jit(solution)/shard_map/reduce_scatter | solution.py:63
  108.9 200.3 %copy-start.3 = (bf16[1,256,384]{2,1,0:T(8,128)(2,1)S(1)}, bf16[1,256,384]{2,1,0:T(8,128)(2,1)}, u32[]{:S(2)}) copy-start(bf16[1,256,384]{2,1,0:T(8,128)(2,1)} %param.11) | copy-start | bytes 589828
  109.0 200.3 %all-gather.4.cloned.1.call-start = ((), (), s32[]{:S(2)}) async-start(), calls=%async_computation.3 | async-start | bytes 1462272 | tf_op jit(solution)/shard_map/all_gather | solution.py:67
  313.1 10.5 %copy-start.4 = (s32[288,2]{0,1:T(2,128)S(1)}, s32[288,2]{0,1:T(2,128)}, u32[]{:S(2)}) copy-start(s32[288,2]{0,1:T(2,128)} %param.7) | copy-start | bytes 6916
  313.1 10.5 %copy-start.5 = (f32[288,2]{0,1:T(2,128)S(1)}, f32[288,2]{0,1:T(2,128)}, u32[]{:S(2)}) copy-start(f32[288,2]{0,1:T(2,128)} %param.8) | copy-start | bytes 6916
  313.2 64.8 %all-to-all-start = ((bf16[32,81,384]{2,1,0:T(8,128)(2,1)}), bf16[32,81,384]{2,1,0:T(8,128)(2,1)S(1)}, u32[]{:S(2)}, u32[]{:S(2)}) async-start(bf16[32,81,384]{2,1,0:T(8,128)(2,1)} %reshape.310), calls=%async_computation.1 | async-start | bytes 4325376 | tf_op jit(solution)/shard_map/all_to_all | solution.py:70
Sparse Core Ops, SparseCore 0:
  13.3 89.1 all-gather.5
  109.1 125.3 reduce-scatter.1
  236.8 72.4 all-gather.3
where the time goes:
time: 386 us
  waiting for transfers between devices  342 us (89%)
  between operations  13.2 us (3%)
  starting transfers between devices  10.5 us (3%)
  local copies, waits for them, and re-layouts  8.17 us (2%)
  other arithmetic  7.01 us (2%)
  matrix products  5.01 us (1%)
    reduce_scatter x1, waiting for transfers between devices, local(): summed = lax.psum_scatter(partial, 'fsdp', scatter_dimension=0, tiled=True)  125 us
    all_gather x1, waiting for transfers between devices, local(): selected = lax.all_gather(own_slots, 'ed', axis=0, tiled=True)  89.2 us
    all_gather x1, waiting for transfers between devices, local(): act_rows = lax.all_gather(activation, 'fsdp', axis=0, tiled=True)[:rows]  73.1 us
    all_to_all x1, waiting for transfers between devices, local(): lax.all_to_all(term, 'ed', split_axis=0, concat_axis=0, tiled=True)  54.3 us
    all_to_all x1, starting transfers between devices, local(): lax.all_to_all(term, 'ed', split_axis=0, concat_axis=0, tiled=True)  10.5 us
  transfers between devices with their start and end apart: 4, of which 4 were waited for; matrix products, arithmetic and copies ran while one was open for 0% of the time, Pallas kernels for 0%

commit v1 on v0

--- a/solution.py
+++ b/solution.py
@@ -53,7 +53,10 @@
     hidden_dev = w_gate.shape[2]
     n_ed = lax.axis_size("ed")
     own_slots = pick_rows(tokens[None], expert_ids[None], window, CAP)[0, 0]
-    selected = lax.all_gather(own_slots, "ed", axis=0, tiled=True)
+    count = lax.axis_size("ed")
+    tiles = jnp.stack([own_slots for _ in range(count)])
+    tiles = lax.all_to_all(tiles, "ed", split_axis=0, concat_axis=0)
+    selected = jnp.concatenate(tiles, axis=0)
     both = jnp.concatenate([w_gate[0], w_up[0]], axis=1)
     partial = jnp.dot(selected, both, preferred_element_type=jnp.float32)
     n_fsdp = lax.axis_size("fsdp")

time: 386 us -> 362 us (0.938)
  waiting for transfers between devices: 342 us -> 251 us
  blocking collectives: 0 us -> 66.9 us
    all_gather x1 -> x0, waiting for transfers between devices: 89.2 us -> none  [local(): selected = lax.all_gather(own_slots, 'ed', axis=0, tiled=True)]
    all_to_all x0 -> x1, blocking collectives: none -> 66.9 us  [local(): tiles = lax.all_to_all(tiles, 'ed', split_axis=0, concat_axis=0)]
  transfers between devices with their start and end apart: 4 -> 3, of which waited for: 4 -> 3; matrix products, arithmetic and copies ran while one was open for 0% -> 0% of each run, Pallas kernels for 0% -> 0%
where the time goes in v1:
time: 362 us; the launch traced here: 361 us
  waiting for transfers between devices  251 us (69%)
  blocking collectives  66.9 us (18%)
  between operations  13.5 us (4%)
  starting transfers between devices  10.5 us (3%)
  local copies, waits for them, and re-layouts  8.41 us (2%)
  other arithmetic  6.38 us (2%)
  matrix products  5.01 us (1%)
    reduce_scatter x1, waiting for transfers between devices, local(): summed = lax.psum_scatter(partial, 'fsdp', scatter_dimension=0, tiled=True)  123 us
    all_gather x1, waiting for transfers between devices, local(): act_rows = lax.all_gather(activation, 'fsdp', axis=0, tiled=True)[:rows]  73.1 us
    all_to_all x1, blocking collectives, local(): tiles = lax.all_to_all(tiles, 'ed', split_axis=0, concat_axis=0)  66.9 us
    all_to_all x1, waiting for transfers between devices, local(): lax.all_to_all(term, 'ed', split_axis=0, concat_axis=0, tiled=True)  54.3 us
    all_to_all x1, starting transfers between devices, local(): lax.all_to_all(term, 'ed', split_axis=0, concat_axis=0, tiled=True)  10.5 us
  transfers between devices with their start and end apart: 3, of which 3 were waited for; matrix products, arithmetic and copies ran while one was open for 0% of the time, Pallas kernels for 0%

profile of v1, /device:TPU:64, one launch (start us, length us, event | category | flops | bytes accessed | tf_op | source)
XLA Modules:
  0.0 361.2 jit_solution(5139383004858369607)
XLA Ops:
  6.5 0.7 fusion.18
  7.3 0.3 reduce-window.6
  7.6 0.2 slice_reduce_fusion
  7.8 0.2 reduce-window.9
  8.0 0.1 broadcast.185
  8.1 3.0 convert_reduce_fusion.1
  11.1 1.3 gather_fusion
  12.4 0.1 select_select_fusion
  12.5 0.2 stack.3
  12.7 66.9 %all_to_all.10 = bf16[32,81,384]{2,1,0:T(8,128)(2,1)} all-to-all(bf16[32,81,384]{2,1,0:T(8,128)(2,1)S(1)} %stack.3), channel_id=1, replica_groups=mesh['fsdp'=16,'ed'=32] {'ed'}, dimensions={0} | all-to-all | bytes 3981312 | tf_op jit(solution)/shard_map/all_to_all | solution.py:58
  79.6 1.9 reshape.314
  81.6 1.5 fusion.1
  83.1 3.0 pad.9
  86.1 0.0 reduce-scatter.2.cloned.1.call-update
  86.1 0.0 all-gather.2.cloned.1.call-start
  86.2 123.1 %reduce-scatter.2.cloned.1.call-done = f32[168,512]{1,0:T(8,128)} async-done(((f32[2688,512]{1,0:T(8,128)}), f32[168,512]{1,0:T(8,128)}) %reduce-scatter.2.cloned.1.call-update) | async-done | bytes 344080 | tf_op jit(solution)/shard_map/reduce_scatter | solution.py:66
  209.2 1.7 fusion.6
  211.0 73.1 %all-gather.2.cloned.1.call-done = bf16[2688,256]{1,0:T(8,128)(2,1)} async-done(((bf16[168,256]{1,0:T(8,128)(2,1)}), bf16[2688,256]{1,0:T(8,128)(2,1)}) %all-gather.2.cloned.1.call-update) | async-done | bytes 1376272 | tf_op jit(solution)/shard_map/all_gather | solution.py:70
  284.0 2.2 convolution_convert_fusion
  286.2 1.7 reshape.315
  287.9 10.5 %all-to-all-start.1 = ((bf16[32,81,384]{2,1,0:T(8,128)(2,1)}), bf16[32,81,384]{2,1,0:T(8,128)(2,1)S(1)}, u32[]{:S(2)}, u32[]{:S(2)}) async-start(bf16[32,81,384]{2,1,0:T(8,128)(2,1)} %reshape.315), calls=%async_computation.2 | async-start | bytes 4325376 | tf_op jit(solution)/shard_map/all_to_all | solution.py:73
  298.4 54.3 %all-to-all-done.1 = bf16[32,81,384]{2,1,0:T(8,128)(2,1)S(1)} async-done(((bf16[32,81,384]{2,1,0:T(8,128)(2,1)}), bf16[32,81,384]{2,1,0:T(8,128)(2,1)S(1)}, u32[]{:S(2)}, u32[]{:S(2)}) %all-to-all-start.1) | async-done | bytes 1990688 | tf_op jit(solution)/shard_map/all_to_all | solution.py:73
  352.7 0.3 convert_reduce_fusion
  353.0 1.3 convolution_convert_fusion.1
  (25 shorter events, 0.2 us)
Async XLA Ops:
  6.5 4.6 %copy-start = (bf16[288,384]{1,0:T(8,128)(2,1)S(1)}, bf16[288,384]{1,0:T(8,128)(2,1)}, u32[]{:S(2)}) copy-start(bf16[288,384]{1,0:T(8,128)(2,1)} %param.6) | copy-start | bytes 663556
  6.5 202.7 %reduce-scatter.2.cloned.1.call-start = ((), (), s32[]{:S(2)}) async-start(), calls=%async_computation.3 | async-start | bytes 5849088 | tf_op jit(solution)/shard_map/reduce_scatter | solution.py:66
  79.6 1.9 copy-start.1
  79.6 2.0 copy-start.2
  86.1 197.9 %copy-start.3 = (bf16[1,256,384]{2,1,0:T(8,128)(2,1)S(1)}, bf16[1,256,384]{2,1,0:T(8,128)(2,1)}, u32[]{:S(2)}) copy-start(bf16[1,256,384]{2,1,0:T(8,128)(2,1)} %param.11) | copy-start | bytes 589828
  86.1 197.9 %all-gather.2.cloned.1.call-start = ((), (), s32[]{:S(2)}) async-start(), calls=%async_computation.4 | async-start | bytes 1462272 | tf_op jit(solution)/shard_map/all_gather | solution.py:70
  287.9 10.5 %copy-start.4 = (s32[288,2]{0,1:T(2,128)S(1)}, s32[288,2]{0,1:T(2,128)}, u32[]{:S(2)}) copy-start(s32[288,2]{0,1:T(2,128)} %param.7) | copy-start | bytes 6916
  287.9 10.5 %copy-start.5 = (f32[288,2]{0,1:T(2,128)S(1)}, f32[288,2]{0,1:T(2,128)}, u32[]{:S(2)}) copy-start(f32[288,2]{0,1:T(2,128)} %param.8) | copy-start | bytes 6916
  287.9 64.8 %all-to-all-start.1 = ((bf16[32,81,384]{2,1,0:T(8,128)(2,1)}), bf16[32,81,384]{2,1,0:T(8,128)(2,1)S(1)}, u32[]{:S(2)}, u32[]{:S(2)}) async-start(bf16[32,81,384]{2,1,0:T(8,128)(2,1)} %reshape.315), calls=%async_computation.2 | async-start | bytes 4325376 | tf_op jit(solution)/shard_map/all_to_all | solution.py:73
Sparse Core Ops, SparseCore 0:
  86.2 122.9 reduce-scatter.1
  211.5 72.4 all-gather.1
